TPU v7x, 128 devices: a whole 4x4x4 slice. The times are simulated.
128 devices in a mesh: pair: 8 (over y, z_lo), virt: 16 (over z_hi, x, core).
Axes of the slice: x: 4, y: 4, z: 4 (z_hi: 2, z_lo: 2; z = z_hi * 2 + z_lo), core: 2. Of those that a mesh axis runs over, the one named last changes fastest.
Arguments:
- amplitudes: float32 [4096, 16384], P('pair', 'virt'), may hold values from -6 to 6
- integrals: bfloat16 [16384, 16384], P('pair', 'virt'), may hold values from -0.046875 to 0.046875
- occ_energy: float32 [4096], P('pair'), may hold values from 0.5 to 4
- vir_energy: float32 [16384], P('virt'), may hold values from 0.5 to 4
- tile_mask: int32 [512, 128], P('pair', 'virt'), may hold values 0 or 1
- partner_slot: int32 [512, 128], P('pair', 'virt'), may hold values from 0 to 127, as said below
Outputs:
- new_amplitudes: float32 [4096, 16384], P('pair', 'virt')
Inputs may be any that keep to these rules, and one draw needn't show every extreme that they name: `partner_slot`: within the block of tiles of each device (tile rows of one pair index by tile columns of one virt index), every device number 0 to 127 stands exactly 4 times, in an order drawn from the seed.
All inputs are finite; a program needn't handle non-finite values. No bound on the sum of `tile_mask` on one device may be relied on, other than what follows from the above.
Results may differ from a plain program's by a relative error of at most 0.0012.
Values may be sent and summed in bfloat16 or wider, within the bound.
No kernel may reach another device: no remote copies, remote signals or barrier semaphores. Data moves between devices by JAX's collectives and lax.ppermute only.
A program may use at most 128 MiB of HBM per device.

v0:
```python
import jax
import jax.numpy as jnp
from jax import lax
from jax.sharding import PartitionSpec as P

TR = 8
TC = 128


def shards(amplitudes, integrals, occ_energy, vir_energy, tile_mask, partner_slot):
    row_count, col_count = amplitudes.shape
    amp_half = amplitudes.astype(jnp.bfloat16)
    pair_count = lax.axis_size("pair")
    virt_count = lax.axis_size("virt")
    full_panels = lax.all_gather(amp_half, "virt", axis=1, tiled=True)
    ladder = jnp.dot(
        full_panels,
        lax.all_gather(integrals, "pair", axis=0, tiled=True),
        preferred_element_type=jnp.float32,
    )
    row_tiles = row_count // TR
    col_tiles = col_count // TC
    tile_total = row_tiles * col_tiles
    weights = tile_mask.astype(jnp.float32)
    masked = ladder.reshape(row_tiles, TR, col_tiles, TC) * weights[:, None, :, None]
    tiles = masked.transpose(0, 2, 1, 3).reshape(tile_total, TR * TC)
    slots = partner_slot.reshape(tile_total)
    ordering = jnp.argsort(slots, stable=True)
    inverse = jnp.argsort(ordering, stable=True)
    device_count = pair_count * virt_count
    per_peer = tile_total // device_count
    outgoing = jnp.take(tiles, ordering, axis=0)
    incoming = lax.all_to_all(
        outgoing.reshape(device_count, per_peer, TR * TC),
        ("pair", "virt"),
        split_axis=0,
        concat_axis=0,
        tiled=True,
    )
    partner = jnp.take(incoming.reshape(tile_total, TR * TC), inverse, axis=0)
    symmetric = (
        (tiles + partner)
        .reshape(row_tiles, col_tiles, TR, TC)
        .transpose(0, 2, 1, 3)
        .reshape(row_count, col_count)
    )
    denominator = occ_energy[:, None] + vir_energy[None, :]
    return amplitudes - symmetric / denominator


def solution(mesh):
    in_specs = (
        P("pair", "virt"),
        P("pair", "virt"),
        P("pair"),
        P("virt"),
        P("pair", "virt"),
        P("pair", "virt"),
    )
    out_specs = P("pair", "virt")
    return jax.shard_map(shards, mesh=mesh, in_specs=in_specs, out_specs=out_specs, check_vma=False)
```

profile of v0, /device:TPU:1, one launch (start us, length us, event | category | flops | bytes accessed | tf_op | source)
XLA Modules:
  0.0 852.6 jit_solution(5119973933379959296)
XLA Ops:
  6.5 0.0 all-gather.3.cloned.1.call-start
  6.5 2.7 convert_element_type.6
  9.3 0.0 all-gather.3.cloned.1.call-update
  9.3 0.0 copy-start.4
  9.3 0.0 copy-start.3
  9.3 0.0 all-gather.5.cloned.1.call-start
  9.4 0.7 all-gather.5.cloned.1.call-update
  10.1 0.0 copy-done.4
  10.1 0.1 copy.8
  10.2 0.0 copy-done.3
  10.2 0.1 copy.9
  10.3 0.1 reshape.31
  10.4 3.8 sort.31
  14.2 109.1 %all-gather.3.cloned.1.call-done = bf16[512,16384]{1,0:T(8,128)(2,1)} async-done(((bf16[512,1024]{1,0:T(8,128)(2,1)}), bf16[512,16384]{1,0:T(8,128)(2,1)}) %all-gather.3.cloned.1.call-update) | async-done | bytes 16777232 | tf_op jit(solution)/shard_map/all_gather | solution.py:15
  123.3 638.9 %all-gather.5.cloned.1.call-done = bf16[16384,1024]{1,0:T(8,128)(2,1)} async-done(((bf16[2048,1024]{1,0:T(8,128)(2,1)}), bf16[16384,1024]{1,0:T(8,128)(2,1)}) %all-gather.5.cloned.1.call-update) | async-done | bytes 33554448 | tf_op jit(solution)/shard_map/all_gather | solution.py:18
  762.1 27.1 %fusion.1 = f32[64,8,8,128]{3,2,1,0:T(8,128)S(1)} fusion(bf16[512,16384]{1,0:T(8,128)(2,1)} %all-gather.3.cloned.1.call-done, bf16[16384,1024]{1,0:T(8,128)(2,1)} %all-gather.5.cloned.1.call-done, f32[64,8]{1,0:T(8,128)S(1)} %copy.8), kind=kOutput, calls=%fused_computation.6 | convolution fusion | flops 17180393472 | bytes 52430848 | tf_op jit(solution)/shard_map/dot_general | solution.py:16
  789.3 0.0 copy-start.1
  789.3 0.5 copy.16
  789.8 0.9 copy-done.1
  790.6 2.6 gather_fusion
  793.3 1.8 broadcast_select_fusion
  795.1 1.6 reshape.32
  796.7 9.9 %all-to-all-start = ((f32[128,4,1024]{2,1,0:T(4,128)}), f32[128,4,1024]{2,1,0:T(4,128)}, u32[]{:S(2)}, u32[]{:S(2)}) async-start(f32[128,4,1024]{2,1,0:T(4,128)} %reshape.32), calls=%async_computation | async-start | bytes 4194304 | tf_op jit(solution)/shard_map/all_to_all | solution.py:33
  806.6 3.8 sort.32
  810.4 26.0 %all-to-all-done = f32[128,4,1024]{2,1,0:T(4,128)} async-done(((f32[128,4,1024]{2,1,0:T(4,128)}), f32[128,4,1024]{2,1,0:T(4,128)}, u32[]{:S(2)}, u32[]{:S(2)}) %all-to-all-start) | async-done | bytes 2097184 | tf_op jit(solution)/shard_map/all_to_all | solution.py:33
  836.4 2.0 reshape.33
  838.4 2.7 gather_fusion.1
  841.0 0.0 copy-start
  841.0 0.0 copy-start.2
  841.0 0.0 copy-start.5
  841.0 2.9 fusion.2
  843.9 0.0 copy-done
  843.9 0.0 copy-done.2
  843.9 0.0 copy-done.5
  843.9 1.9 fusion
  (9 shorter events, 0.0 us)
Async XLA Ops:
  6.5 116.7 %all-gather.3.cloned.1.call-start = ((), (), s32[]{:S(2)}) async-start(), calls=%async_computation.1 | async-start | bytes 17825792 | tf_op jit(solution)/shard_map/all_gather | solution.py:15
  9.3 0.8 copy-start.4
  9.3 0.9 copy-start.3
  9.3 752.8 %all-gather.5.cloned.1.call-start = ((), (), s32[]{:S(2)}) async-start(), calls=%async_computation.2 | async-start | bytes 37748736 | tf_op jit(solution)/shard_map/all_gather | solution.py:18
  789.3 1.4 copy-start.1
  796.7 39.7 %all-to-all-start = ((f32[128,4,1024]{2,1,0:T(4,128)}), f32[128,4,1024]{2,1,0:T(4,128)}, u32[]{:S(2)}, u32[]{:S(2)}) async-start(f32[128,4,1024]{2,1,0:T(4,128)} %reshape.32), calls=%async_computation | async-start | bytes 4194304 | tf_op jit(solution)/shard_map/all_to_all | solution.py:33
  841.0 2.9 copy-start
  841.0 2.9 copy-start.2
  841.0 2.9 copy-start.5
Sparse Core Ops, SparseCore 0:
  9.8 113.4 all-gather.2
  124.9 637.1 all-gather.4
where the time goes:
time: 853 us
  waiting for transfers between devices  775 us (91%)
  matrix products  27.1 us (3%)
  other arithmetic  16.9 us (2%)
  between operations  13.5 us (2%)
  local copies, waits for them, and re-layouts  10.5 us (1%)
  starting transfers between devices  9.9 us (1%)
    all_gather x1, waiting for transfers between devices, shards(): lax.all_gather(integrals, 'pair', axis=0, tiled=True)  639 us
    all_gather x1, waiting for transfers between devices, shards(): full_panels = lax.all_gather(amp_half, 'virt', axis=1, tiled=True)  109 us
    dot_general x1, matrix products, shards(): jnp.dot(full_panels, lax.all_gather(integrals, 'pair', axis=0, tiled=True...  27.1 us
    all_to_all x1, waiting for transfers between devices, shards(): lax.all_to_all(outgoing.reshape(device_count, per_peer, TR * TC), ('pair'...  26 us
  transfers between devices with their start and end apart: 3, of which 3 were waited for; matrix products, arithmetic and copies ran while one was open for 1% of the time, Pallas kernels for 0%

commit v1 on v0

--- a/solution.py
+++ b/solution.py
@@ -12,7 +12,8 @@
     amp_half = amplitudes.astype(jnp.bfloat16)
     pair_count = lax.axis_size("pair")
     virt_count = lax.axis_size("virt")
-    full_panels = lax.all_gather(amp_half, "virt", axis=1, tiled=True)
+    sent = jnp.stack([amp_half] * lax.axis_size("virt"))
+    full_panels = jnp.concatenate(lax.all_to_all(sent, "virt", 0, 0), axis=1)
     ladder = jnp.dot(
         full_panels,
         lax.all_gather(integrals, "pair", axis=0, tiled=True),

time: 853 us -> 967 us (1.13)
  local copies, waits for them, and re-layouts: 10.5 us -> 107 us
  waiting for transfers between devices: 775 us -> 786 us
    all_to_all x0 -> x1, waiting for transfers between devices: none -> 300 us  [shards(): full_panels = jnp.concatenate(lax.all_to_all(sent, 'virt', 0, 0), axis=1)]
    all_gather x1, waiting for transfers between devices: 639 us -> 459 us  [shards(): lax.all_gather(integrals, 'pair', axis=0, tiled=True)]
    all_gather x1 -> x0, waiting for transfers between devices: 109 us -> none  [shards(): full_panels = lax.all_gather(amp_half, 'virt', axis=1, tiled=True)]
    dot_general x0 -> x2, local copies, waits for them, and re-layouts: none -> 69.7 us  [shards(): jnp.dot(full_panels, lax.all_gather(integrals, 'pair', axis=0, tiled=True...]
    reshape x0 -> x1, local copies, waits for them, and re-layouts: none -> 18.7 us  [shards(): full_panels = jnp.concatenate(lax.all_to_all(sent, 'virt', 0, 0), axis=1)]
  transfers between devices with their start and end apart: 3 -> 3, of which waited for: 3 -> 3; matrix products, arithmetic and copies ran while one was open for 1% -> 6% of each run, Pallas kernels for 0% -> 0%
where the time goes in v1:
time: 967 us; the launch traced here: 965 us
  waiting for transfers between devices  786 us (81%)
  local copies, waits for them, and re-layouts  107 us (11%)
  matrix products  24.8 us (3%)
  starting transfers between devices  19.1 us (2%)
  other arithmetic  15.4 us (2%)
  between operations  13.5 us (1%)
    all_gather x1, waiting for transfers between devices, shards(): lax.all_gather(integrals, 'pair', axis=0, tiled=True)  459 us
    all_to_all x1, waiting for transfers between devices, shards(): full_panels = jnp.concatenate(lax.all_to_all(sent, 'virt', 0, 0), axis=1)  300 us
    dot_general x2, local copies, waits for them, and re-layouts, shards(): jnp.dot(full_panels, lax.all_gather(integrals, 'pair', axis=0, tiled=True...  69.7 us
    all_to_all x1, waiting for transfers between devices, shards(): lax.all_to_all(outgoing.reshape(device_count, per_peer, TR * TC), ('pair'...  26 us
    dot_general x1, matrix products, shards(): jnp.dot(full_panels, lax.all_gather(integrals, 'pair', axis=0, tiled=True...  24.8 us
  transfers between devices with their start and end apart: 3, of which 3 were waited for; matrix products, arithmetic and copies ran while one was open for 6% of the time, Pallas kernels for 0%

profile of v1, /device:TPU:1, one launch (start us, length us, event | category | flops | bytes accessed | tf_op | source)
XLA Modules:
  0.0 965.1 jit_solution(13276750915044412764)
XLA Ops:
  6.5 0.0 copy-start
  6.5 0.0 all-gather.2.cloned.1.call-start
  6.5 0.7 all-gather.2.cloned.1.call-update
  7.3 0.9 copy-done
  8.1 0.2 convert_element_type.6
  8.3 6.0 stack.2
  14.3 0.0 copy-start.7
  14.3 0.0 copy-start.6
  14.3 9.2 all-to-all-start
  23.5 0.0 copy-done.7
  23.5 0.1 copy.14
  23.6 0.0 copy-done.6
  23.6 0.1 copy.15
  23.7 0.1 reshape.38
  23.8 3.8 sort.31
  27.6 0.0 copy-start.2
  27.6 0.6 pad_clamp_fusion.1
  28.2 0.6 compare_and_fusion.1
  28.8 300.4 %all-to-all-done = bf16[16,512,1024]{2,1,0:T(8,128)(2,1)} async-done(((bf16[16,512,1024]{2,1,0:T(8,128)(2,1)}), bf16[16,512,1024]{2,1,0:T(8,128)(2,1)}, u32[]{:S(2)}, u32[]{:S(2)}) %all-to-all-start) | async-done | bytes 16777248 | tf_op jit(solution)/shard_map/all_to_all | solution.py:16
  329.2 18.7 %copy.12 = bf16[512,16,1024]{2,1,0:T(8,128)(2,1)} copy(bf16[512,16,1024]{2,0,1:T(8,128)(2,1)} %bitcast) | data formatting | bytes 33554432 | tf_op jit(solution)/shard_map/reshape | solution.py:16
  347.9 0.0 copy-done.2
  347.9 25.7 %reshape.65 = bf16[64,8,16384,1]{2,1,0,3:T(8,128)(2,1)} reshape(bf16[512,16,1024]{2,1,0:T(8,128)(2,1)} %copy.12) | data formatting | bytes 33554432 | tf_op jit(solution)/shard_map/dot_general | solution.py:17
  373.5 458.5 %all-gather.2.cloned.1.call-done = bf16[16384,1024]{1,0:T(8,128)(2,1)} async-done(((bf16[2048,1024]{1,0:T(8,128)(2,1)}), bf16[16384,1024]{1,0:T(8,128)(2,1)}) %all-gather.2.cloned.1.call-update) | async-done | bytes 33554448 | tf_op jit(solution)/shard_map/all_gather | solution.py:19
  832.1 44.0 %copy.13 = bf16[1024,16384]{1,0:T(8,128)(2,1)} copy(bf16[1024,16384]{0,1:T(8,128)(2,1)} %bitcast.31) | data formatting | bytes 67108864 | tf_op jit(solution)/shard_map/dot_general | solution.py:17
  876.1 24.8 %multiply_bitcast_fusion = f32[64,8,8,128]{3,2,1,0:T(8,128)} fusion(bf16[8,128,16384,1]{2,1,0,3:T(8,128)(2,1)} %bitcast.32, bf16[64,8,16384,1]{2,1,0,3:T(8,128)(2,1)} %reshape.65, f32[64,8]{1,0:T(8,128)S(1)} %copy.14), kind=kOutput, calls=%fused_computation.9 | convolution fusion | flops 17180393472 | bytes 52430848 | tf_op jit(solution)/shard_map/dot_general | solution.py:17
  900.9 0.0 copy-start.4
  900.9 2.1 copy.23
  903.0 0.0 copy-done.4
  903.0 0.0 copy-start.9
  903.0 2.7 gather_fusion
  905.7 0.0 copy-done.9
  905.7 1.8 broadcast_select_fusion
  907.5 1.6 reshape.39
  909.1 0.0 copy-start.3
  909.1 9.9 %all-to-all-start.1 = ((f32[128,4,1024]{2,1,0:T(4,128)}), f32[128,4,1024]{2,1,0:T(4,128)}, u32[]{:S(2)}, u32[]{:S(2)}) async-start(f32[128,4,1024]{2,1,0:T(4,128)} %reshape.39), calls=%async_computation.1 | async-start | bytes 4194304 | tf_op jit(solution)/shard_map/all_to_all | solution.py:34
  919.0 0.0 copy-done.3
  919.0 3.8 sort.32
  922.8 26.0 %all-to-all-done.1 = f32[128,4,1024]{2,1,0:T(4,128)} async-done(((f32[128,4,1024]{2,1,0:T(4,128)}), f32[128,4,1024]{2,1,0:T(4,128)}, u32[]{:S(2)}, u32[]{:S(2)}) %all-to-all-start.1) | async-done | bytes 2097184 | tf_op jit(solution)/shard_map/all_to_all | solution.py:34
  948.8 2.0 reshape.40
  950.8 2.7 gather_fusion.1
  953.5 0.0 copy-start.1
  953.5 0.0 copy-start.5
  953.5 0.0 copy-start.8
  953.5 2.9 fusion.3
  956.4 0.0 copy-done.1
  956.4 0.0 copy-done.5
  956.4 0.0 copy-done.8
  956.4 1.9 fusion.2
  (7 shorter events, 0.0 us)
Async XLA Ops:
  6.5 1.6 copy-start
  6.5 825.5 %all-gather.2.cloned.1.call-start = ((), (), s32[]{:S(2)}) async-start(), calls=%async_computation.2 | async-start | bytes 37748736 | tf_op jit(solution)/shard_map/all_gather | solution.py:19
  14.3 9.3 copy-start.7
  14.3 9.4 copy-start.6
  14.3 314.9 %all-to-all-start = ((bf16[16,512,1024]{2,1,0:T(8,128)(2,1)}), bf16[16,512,1024]{2,1,0:T(8,128)(2,1)}, u32[]{:S(2)}, u32[]{:S(2)}) async-start(bf16[16,512,1024]{2,1,0:T(8,128)(2,1)} %stack.2), calls=%async_computation | async-start | bytes 33554432 | tf_op jit(solution)/shard_map/all_to_all | solution.py:16
  27.6 320.3 %copy-start.2 = (s32[512]{0:T(512)}, s32[512]{0:T(512)S(1)}, u32[]{:S(2)}) copy-start(s32[512]{0:T(512)S(1)} %get-tuple-element.8) | copy-start | bytes 6148
  900.9 2.1 copy-start.4
  903.0 2.7 copy-start.9
  909.1 9.9 %copy-start.3 = (s32[512]{0:T(512)S(1)}, s32[512]{0:T(512)}, u32[]{:S(2)}) copy-start(s32[512]{0:T(512)} %copy-done.2) | copy-start | bytes 6148
  909.1 39.7 %all-to-all-start.1 = ((f32[128,4,1024]{2,1,0:T(4,128)}), f32[128,4,1024]{2,1,0:T(4,128)}, u32[]{:S(2)}, u32[]{:S(2)}) async-start(f32[128,4,1024]{2,1,0:T(4,128)} %reshape.39), calls=%async_computation.1 | async-start | bytes 4194304 | tf_op jit(solution)/shard_map/all_to_all | solution.py:34
  953.5 2.9 copy-start.1
  953.5 2.9 copy-start.5
  953.5 2.9 copy-start.8
Sparse Core Ops, SparseCore 0:
  9.0 823.0 all-gather.1
